TPU v7x, 32 devices: a whole 2x2x4 slice. The times are simulated.
32 devices in a mesh: groups: 2 (over y), pos: 4 (over z), strand: 2 (over core), heads: 2 (over x).
Axes of the slice: x: 2, y: 2, z: 4, core: 2. Of those that a mesh axis runs over, the one named last changes fastest.
Arguments:
- base_codes: int32 [131072], P(('groups', 'pos')), parts along dimension 0, may hold values from 0 to 3
- embed_table: bfloat16 [512, 1536], P(None, 'heads'), may hold values from -0.5 to 0.5
- attn_gain: float32 [1536], replicated, may hold values from 0.1 to 1.9
- w_query: bfloat16 [1536, 1024], P(None, 'heads')
- w_key: bfloat16 [1536, 128], P(None, 'heads')
- w_value: bfloat16 [1536, 192], P(None, 'heads'), may hold values from -0.15625 to 0.15625
- w_out: bfloat16 [1536, 1536], P('heads'), may hold values from -0.15625 to 0.15625
- head_gain: float32 [1536], replicated, may hold values from 0.1 to 1.9
- w_tracks: bfloat16 [1536, 2, 1536], P(None, None, 'heads'), may hold values from -0.15625 to 0.15625
- track_pairs: int32 [3072], P(('strand', 'heads')), may hold values from 0 to 3071, as said below
Outputs:
- tracks_out: float32 [1024, 3072], P(('groups', 'pos'), ('strand', 'heads')), parts along dimension 0
There are 2 independent parts, one for each index of `groups`. A program takes and returns all parts, laid end to end along the dimension named above; an argument that names none is the same for every part. Nothing has to cross between parts.
Inputs may be any that keep to these rules, and one draw needn't show every extreme that they name: track_pairs is an involution: each aligned pair of tracks 2 j and 2 j + 1 is either swapped or left in place.
All inputs are finite; a program needn't handle non-finite values.
Results may differ from a plain program's by a relative error of at most 0.008.
Values may be sent and summed in bfloat16 or wider, within the bound.
A program may use at most 64 MiB of HBM per device.

v0:
```python
import functools
import math

import jax
import jax.numpy as jnp
from jax import lax
from jax.experimental import pallas as pl
from jax.experimental.pallas import tpu as pltpu
from jax.sharding import PartitionSpec as P

KDIM = 128
VDIM = 192
BIN = 128
F32 = jnp.float32
BF16 = jnp.bfloat16
MESH = pl.DeviceIdType.MESH
NT = (((1,), (1,)), ((), ()))


def spread(table, first, count):
    return jnp.concatenate([table[first + i : first + i + 1, :] for i in range(count)], axis=1)


def partner(z, step, N):
    if N & (N - 1):
        return lax.rem(z + step, N)
    bit = 1
    while bit < N:
        if step & bit:
            z = z + bit - 2 * bit * ((z // bit) % 2)
        bit *= 2
    return z


def farthest(z, k, N):
    up = (N - 1 - z - k + N - 1) // N
    return up * (N - 1 - k) + (1 - up) * (k + z - (N - 1))


def kernel(
    H, N, NC, NX,
    codes_hbm, et_hbm, g1_hbm, wq_hbm, wk_hbm, wv_hbm, wo_hbm, g2_hbm, wt_hbm, tp_hbm,
    out_ref, tp_out,
    codes_ref, g1_ref, g2_ref, et, wq, wkv, wo, wraw, wt, xbuf, kvbuf, tabc, tabs, own, psend, precv, lg, snd, rcv,
    wsem, xs, xr, kvs, kvr, kfs, ps, pr, ss, sr,
):
    h = lax.axis_index("heads")
    z = lax.axis_index("pos")
    strand = lax.axis_index("strand")
    rows = codes_hbm.shape[0]
    dl = et.shape[1]
    D = dl * H
    kl = wk_hbm.shape[0]
    kvl = wkv.shape[0]
    lh = wq.shape[1] // KDIM
    cols = wt.shape[2]
    total = rows * N

    hp = [lax.rem(h + i, H) for i in range(1, H)]
    zp = [partner(z, i, N) for i in range(1, N)]
    barrier = pltpu.get_barrier_semaphore()
    for peer in zp:
        pl.semaphore_signal(barrier, inc=1, device_id={"pos": peer}, device_id_type=MESH)
    for peer in hp:
        pl.semaphore_signal(barrier, inc=1, device_id={"heads": peer}, device_id_type=MESH)
    pl.semaphore_signal(barrier, inc=1, device_id={"strand": 1 - strand}, device_id_type=MESH)

    loads = [
        pltpu.make_async_copy(et_hbm, et, wsem.at[0]),
        pltpu.make_async_copy(wk_hbm, wkv.at[pl.ds(0, kl), :], wsem.at[1]),
        pltpu.make_async_copy(wv_hbm, wkv.at[pl.ds(kl, kvl - kl), :], wsem.at[2]),
        pltpu.make_async_copy(wq_hbm, wq, wsem.at[3]),
        pltpu.make_async_copy(wo_hbm, wo, wsem.at[4]),
        pltpu.make_async_copy(wt_hbm, wraw, wsem.at[5]),
        pltpu.make_async_copy(codes_hbm, codes_ref, wsem.at[6]),
        pltpu.make_async_copy(g1_hbm, g1_ref, wsem.at[7]),
        pltpu.make_async_copy(g2_hbm, g2_ref, wsem.at[8]),
        pltpu.make_async_copy(tp_hbm, tp_out, wsem.at[9]),
    ]
    loads[6].start()
    loads[0].start()
    loads[7].start()
    loads[8].start()
    loads[9].start()

    fwd = strand == 0
    width = 4 * BIN
    src_row = lax.broadcasted_iota(jnp.int32, (BIN, width), 0)
    place = lax.broadcasted_iota(jnp.int32, (BIN, width), 1) // 4
    want = jnp.where(fwd, place, BIN - 1 - place)
    expand = (src_row == want).astype(F32).astype(BF16)
    loads[6].wait()
    repeated = jnp.dot(codes_ref[...].astype(F32).astype(BF16), expand, preferred_element_type=F32)
    letter = lax.broadcasted_iota(jnp.int32, (rows, width), 1) % 4
    letter = jnp.where(fwd, letter, 3 - letter).astype(F32)
    onehot = (repeated == letter).astype(F32).astype(BF16)

    loads[0].wait()
    for k in (1, 2, 3, 5, 4):
        loads[k].start()
    xw = dl // NX
    sends = []
    for c in range(NX):
        part = jnp.dot(onehot, et[:, c * xw : (c + 1) * xw], preferred_element_type=F32)
        xbuf[h, c] = part.astype(BF16)
        if c == 0:
            pl.semaphore_wait(barrier, len(hp) + len(zp) + 1)
        for i, peer in enumerate(hp):
            cp = pltpu.make_async_remote_copy(
                xbuf.at[h, c], xbuf.at[h, c], xs.at[i, c], xr.at[h, c],
                device_id={"heads": peer}, device_id_type=MESH,
            )
            cp.start()
            sends.append(cp)

    half = KDIM // 2
    step = -math.log(10000.0) / half
    lane_pos = lax.broadcasted_iota(jnp.int32, (half, rows), 1)
    kinv = jnp.exp(lax.broadcasted_iota(jnp.int32, (half, rows), 0).astype(F32) * step)
    for p in range(N):
        pos = lane_pos + p * rows
        pos = jnp.where(fwd, pos, total - 1 - pos).astype(F32)
        tabc[p] = jnp.cos(pos * kinv)
        tabs[p] = jnp.sin(pos * kinv)
    qpos = lax.broadcasted_iota(jnp.int32, (rows, KDIM), 0) + z * rows
    qpos = jnp.where(fwd, qpos, total - 1 - qpos).astype(F32)
    qlane = lax.broadcasted_iota(jnp.int32, (rows, KDIM), 1)
    qang = qpos * jnp.exp((qlane % half).astype(F32) * step)
    qcos = jnp.cos(qang)
    qsin = jnp.where(qlane < half, -1.0, 1.0) * jnp.sin(qang)

    loads[5].wait()
    for i in range(0, D, 128):
        wt[:, i : i + 128, :] = jnp.swapaxes(wraw[i : i + 128], 0, 1)

    for peer in hp:
        for c in range(NX):
            pltpu.make_async_remote_copy(
                xbuf.at[peer, c], xbuf.at[peer, c], xs.at[0, c], xr.at[peer, c],
                device_id={"heads": peer}, device_id_type=MESH,
            ).wait_recv()
    loads[7].wait()
    loads[8].wait()
    loads[9].wait()
    x = jnp.concatenate([xbuf[i, c] for i in range(H) for c in range(NX)], axis=1)
    xf = x.astype(F32)
    scale = lax.rsqrt(jnp.mean(xf * xf, axis=1, keepdims=True) + 1e-06)
    normed = (xf * scale * spread(g1_ref[...], 0, D // 128)).astype(BF16)

    loads[1].wait()
    loads[2].wait()
    kv_own = lax.dot_general(wkv[...], normed, NT, preferred_element_type=F32)
    kvbuf[z, h] = kv_own.astype(BF16)

    def kv_copy(p, hh, send, target):
        return pltpu.make_async_remote_copy(
            kvbuf.at[p, hh], kvbuf.at[p, hh], send, kvr.at[p, hh],
            device_id=target, device_id_type=MESH,
        )

    for i in range(N - 1):
        cp = kv_copy(z, h, kvs.at[i], {"pos": farthest(z, i, N)})
        cp.start()
        sends.append(cp)
    for i, peer in enumerate(hp):
        cp = kv_copy(z, h, kfs.at[i, 0], {"heads": peer})
        cp.start()
        sends.append(cp)

    loads[3].wait()
    queries = jnp.dot(normed, wq[...], preferred_element_type=F32).astype(BF16).astype(F32)
    rotated = []
    for a in range(lh):
        qa = queries[:, a * KDIM : (a + 1) * KDIM]
        rotated.append((qa * qcos + pltpu.roll(qa, half, 1) * qsin).astype(BF16))

    for j, peer in enumerate(zp):
        kv_copy(peer, h, kvs.at[0], {"pos": peer}).wait_recv()
        for i, other in enumerate(hp):
            cp = kv_copy(peer, h, kfs.at[i, j + 1], {"heads": other})
            cp.start()
            sends.append(cp)
    score_parts, vts = [[] for _ in range(lh)], []
    for p in [z] + zp:
        for other in hp:
            kv_copy(p, other, kfs.at[0, 0], {"heads": other}).wait_recv()
        kt = jnp.concatenate([kvbuf[p, i, :kl, :] for i in range(H)], axis=0).astype(F32)
        lo, hi = kt[:half], kt[half:]
        kt = jnp.concatenate(
            [lo * tabc[p] - hi * tabs[p], hi * tabc[p] + lo * tabs[p]], axis=0
        ).astype(BF16)
        vts.append(jnp.concatenate([kvbuf[p, i, kl:, :] for i in range(H)], axis=0))
        for a in range(lh):
            score_parts[a].append(
                jnp.dot(rotated[a], kt, preferred_element_type=F32) * KDIM ** (-0.5)
            )
    vt = jnp.concatenate(vts, axis=1)
    heads_out = []
    for a in range(lh):
        scores = jnp.concatenate(score_parts[a], axis=1)
        top = jnp.max(scores, axis=1, keepdims=True)
        weights = jnp.exp(scores - top)
        weight_sum = jnp.sum(weights, axis=1, keepdims=True)
        mixed = lax.dot_general(weights.astype(BF16), vt, NT, preferred_element_type=F32)
        heads_out.append(mixed / weight_sum)
    merged = jnp.concatenate(heads_out, axis=1).astype(BF16)

    loads[4].wait()
    cw = D // NC
    for c in range(NC):
        part = jnp.dot(merged, wo[:, c * cw : (c + 1) * cw], preferred_element_type=F32)
        own[c] = part
        psend[c] = part.astype(BF16)
        for i, peer in enumerate(hp):
            cp = pltpu.make_async_remote_copy(
                psend.at[c], precv.at[h, c], ps.at[i, c], pr.at[h, c],
                device_id={"heads": peer}, device_id_type=MESH,
            )
            cp.start()
            sends.append(cp)
    other_strand = 1 - strand
    hr = rows // 2
    swaps = []
    square = jnp.zeros((rows, 1), F32)
    for c in range(NC):
        summed = x[:, c * cw : (c + 1) * cw].astype(F32) + own[c]
        for peer in hp:
            pltpu.make_async_remote_copy(
                psend.at[c], precv.at[peer, c], ps.at[0, c], pr.at[peer, c],
                device_id={"heads": peer}, device_id_type=MESH,
            ).wait_recv()
            summed = summed + precv[peer, c].astype(F32)
        hidden = summed.astype(BF16).astype(F32)
        square = square + jnp.sum(hidden * hidden, axis=1, keepdims=True)
        gained = (hidden * spread(g2_ref[...], c * cw // 128, cw // 128)).astype(BF16)
        last = c == NC - 1
        for s in (other_strand, strand):
            part = jnp.dot(gained, wt[s, c * cw : (c + 1) * cw, :], preferred_element_type=F32)
            if c > 0:
                part = lg[s] + part
            if not last:
                lg[s] = part
                continue
            logits = part * lax.rsqrt(square / D + 1e-06)
            for r in range(2):
                part = logits[r * hr : (r + 1) * hr]
                track = (jnp.maximum(part, 0.0) + jnp.log1p(jnp.exp(-jnp.abs(part)))).astype(BF16)
                if s is strand:
                    out_ref[strand, r * hr : (r + 1) * hr, :] = track
                    continue
                snd[r] = track
                cp = pltpu.make_async_remote_copy(
                    snd.at[r], rcv.at[r], ss.at[r], sr.at[r],
                    device_id={"strand": other_strand}, device_id_type=MESH,
                )
                cp.start()
                sends.append(cp)
                swaps.append(cp)
    for r in range(2):
        swaps[r].wait_recv()
        out_ref[other_strand, r * hr : (r + 1) * hr, :] = rcv[r]
    for cp in sends:
        cp.wait_send()


def average(H, tracks_ref, tp_ref, out_ref):
    cols = out_ref.shape[1]
    pairs = tp_ref[...]
    first = (lax.axis_index("strand") * H + lax.axis_index("heads")) * cols
    lane = lax.broadcasted_iota(jnp.int32, (1, 128), 1)
    for b in range(cols // 128):
        at = slice(b * 128, (b + 1) * 128)
        r = tracks_ref[1, :, at].astype(F32)
        crossed = jnp.where(lane % 2 == 0, pltpu.roll(r, 127, 1), pltpu.roll(r, 1, 1))
        stays = pairs[b : b + 1, :] == first + b * 128 + lane
        r = jnp.where(stays, r, crossed)
        out_ref[:, at] = 0.5 * (tracks_ref[0, :, at].astype(F32) + r)


def body(
    base_codes, embed_table, attn_gain, w_query, w_key, w_value, w_out, head_gain, w_tracks, track_pairs
):
    H = lax.axis_size("heads")
    N = lax.axis_size("pos")
    rows = base_codes.shape[0] // BIN
    dl = embed_table.shape[1]
    D = dl * H
    cols = w_tracks.shape[2]
    kvl = w_key.shape[1] + w_value.shape[1]
    NC, NX = 6, 3
    vm = pl.BlockSpec(memory_space=pltpu.VMEM)
    hbm = pl.BlockSpec(memory_space=pl.ANY)
    dma = pltpu.SemaphoreType.DMA
    hm = max(H - 1, 1)
    zm = max(N - 1, 1)
    tracks, pairs = pl.pallas_call(
        functools.partial(kernel, H, N, NC, NX),
        out_shape=[pltpu.VMEM((2, rows, cols), BF16), pltpu.VMEM((cols // 128, 128), jnp.int32)],
        in_specs=[hbm] * 10,
        out_specs=[vm, vm],
        scratch_shapes=[
            pltpu.VMEM((rows, BIN), jnp.int32),
            pltpu.VMEM((D // 128, 128), F32),
            pltpu.VMEM((D // 128, 128), F32),
            pltpu.VMEM(embed_table.shape, BF16),
            pltpu.VMEM(w_query.shape, BF16),
            pltpu.VMEM((kvl, D), BF16),
            pltpu.VMEM(w_out.shape, BF16),
            pltpu.VMEM(w_tracks.shape, BF16),
            pltpu.VMEM((2, D, cols), BF16),
            pltpu.VMEM((H, NX, rows, dl // NX), BF16),
            pltpu.VMEM((N, H, kvl, rows), BF16),
            pltpu.VMEM((N, KDIM // 2, rows), F32),
            pltpu.VMEM((N, KDIM // 2, rows), F32),
            pltpu.VMEM((NC, rows, D // NC), F32),
            pltpu.VMEM((NC, rows, D // NC), BF16),
            pltpu.VMEM((H, NC, rows, D // NC), BF16),
            pltpu.VMEM((2, rows, cols), F32),
            pltpu.VMEM((2, rows // 2, cols), BF16),
            pltpu.VMEM((2, rows // 2, cols), BF16),
            dma((10,)),
            dma((hm, NX)),
            dma((H, NX)),
            dma((zm,)),
            dma((N, H)),
            dma((hm, N)),
            dma((hm, NC)),
            dma((H, NC)),
            dma((2,)),
            dma((2,)),
        ],
        compiler_params=pltpu.CompilerParams(
            collective_id=0, has_side_effects=True, vmem_limit_bytes=60 * 1024 * 1024
        ),
    )(
        base_codes.reshape(rows, BIN),
        embed_table,
        attn_gain.reshape(D // 128, 128),
        w_query,
        w_key.T,
        w_value.T,
        w_out,
        head_gain.reshape(D // 128, 128),
        w_tracks,
        track_pairs.reshape(cols // 128, 128),
    )
    keep = pltpu.with_memory_space_constraint
    return pl.pallas_call(
        functools.partial(average, H),
        out_shape=jax.ShapeDtypeStruct((rows, cols), F32),
        in_specs=[vm, vm],
        out_specs=vm,
    )(keep(tracks, pltpu.VMEM), keep(pairs, pltpu.VMEM))


def solution(mesh):
    placed = (
        P(("groups", "pos")),
        P(None, "heads"),
        P(),
        P(None, "heads"),
        P(None, "heads"),
        P(None, "heads"),
        P("heads", None),
        P(),
        P(None, None, "heads"),
        P(("strand", "heads")),
    )
    return jax.shard_map(
        body,
        mesh=mesh,
        in_specs=placed,
        out_specs=P(("groups", "pos"), ("strand", "heads")),
        check_vma=False,
    )
```

profile of v0, /device:TPU:0, one launch (start us, length us, event | category | flops | bytes accessed | tf_op | source)
XLA Modules:
  0.0 30.0 jit_solution(6406366226558616308)
XLA Ops:
  0.0 29.1 %shard_map.100 = (bf16[2,128,768]{2,1,0:T(8,128)(2,1)S(1)}, s32[6,128]{1,0:T(8,128)S(1)}) custom-call(s32[128,128]{1,0:T(8,128)} %bitcast.8, bf16[512,768]{1,0:T(8,128)(2,1)} %et_hbm.1, f32[12,128]{1,0:T(8,128)} %bitcast.9, bf16[1536,512]{1,0:T(8,128)(2,1)} %wq_hbm.1, bf16[64,1536]{1,0:T(8,128)(2,1)} %bitcast.7, bf16[96,1536]{1,0:T(8,128)(2,1)} %bitcast.6, ...), custom_call_target="tpu_custom_call" | custom-call | tf_op jit(solution)/shard_map/pallas_call | solution.py:296
  29.1 0.9 %shard_map.101 = f32[128,768]{1,0:T(8,128)} custom-call(bf16[2,128,768]{2,1,0:T(8,128)(2,1)S(1)} %get-tuple-element.7.tracks_ref, s32[6,128]{1,0:T(8,128)S(1)} %get-tuple-element.8.tp_ref), custom_call_target="tpu_custom_call" | custom-call | tf_op jit(solution)/shard_map/pallas_call | solution.py:348
where the time goes:
time: 30.2 us; the launch traced here: 30 us
  Pallas kernels  30 us (99%)
    pallas_call x1, Pallas kernels, body(): pl.pallas_call(functools.partial(kernel, H, N, NC, NX), out_shape=[pltpu....  29.1 us
    pallas_call x1, Pallas kernels, body(): pl.pallas_call(functools.partial(average, H), out_shape=jax.ShapeDtypeStr...  0.94 us

commit v1 on v0

--- a/solution.py
+++ b/solution.py
@@ -15,6 +15,7 @@
 BF16 = jnp.bfloat16
 MESH = pl.DeviceIdType.MESH
 NT = (((1,), (1,)), ((), ()))
+FIRST = 1
 
 
 def spread(table, first, count):
@@ -42,7 +43,7 @@
     codes_hbm, et_hbm, g1_hbm, wq_hbm, wk_hbm, wv_hbm, wo_hbm, g2_hbm, wt_hbm, tp_hbm,
     out_ref, tp_out,
     codes_ref, g1_ref, g2_ref, et, wq, wkv, wo, wraw, wt, xbuf, kvbuf, tabc, tabs, own, psend, precv, lg, snd, rcv,
-    wsem, xs, xr, kvs, kvr, kfs, ps, pr, ss, sr,
+    wsem, xs, xr, kvs, kvr, kfs, kds, ps, pr, ss, sr, ready, turn,
 ):
     h = lax.axis_index("heads")
     z = lax.axis_index("pos")
@@ -58,12 +59,26 @@
 
     hp = [lax.rem(h + i, H) for i in range(1, H)]
     zp = [partner(z, i, N) for i in range(1, N)]
+    other_strand = 1 - strand
+
+    def direct(p):
+        return (strand != FIRST) | (abs(p - z) == N - 1)
+
     barrier = pltpu.get_barrier_semaphore()
-    for peer in zp:
-        pl.semaphore_signal(barrier, inc=1, device_id={"pos": peer}, device_id_type=MESH)
+
+    def greet(sem, up):
+        for peer in zp:
+            @pl.when(peer > z if up else peer < z)
+            def _():
+                for other in [h] + hp:
+                    pl.semaphore_signal(
+                        sem, inc=1, device_id={"pos": peer, "heads": other}, device_id_type=MESH
+                    )
+
+    greet(barrier, True)
     for peer in hp:
         pl.semaphore_signal(barrier, inc=1, device_id={"heads": peer}, device_id_type=MESH)
-    pl.semaphore_signal(barrier, inc=1, device_id={"strand": 1 - strand}, device_id_type=MESH)
+    pl.semaphore_signal(barrier, inc=1, device_id={"strand": other_strand}, device_id_type=MESH)
 
     loads = [
         pltpu.make_async_copy(et_hbm, et, wsem.at[0]),
@@ -100,18 +115,24 @@
         loads[k].start()
     xw = dl // NX
     sends = []
+
+    def x_copy(i, c):
+        return pltpu.make_async_remote_copy(
+            xbuf.at[h, c], xbuf.at[h, c], xs.at[i, c], xr.at[h, c],
+            device_id={"heads": hp[i]}, device_id_type=MESH,
+        )
+
     for c in range(NX):
         part = jnp.dot(onehot, et[:, c * xw : (c + 1) * xw], preferred_element_type=F32)
         xbuf[h, c] = part.astype(BF16)
         if c == 0:
-            pl.semaphore_wait(barrier, len(hp) + len(zp) + 1)
-        for i, peer in enumerate(hp):
-            cp = pltpu.make_async_remote_copy(
-                xbuf.at[h, c], xbuf.at[h, c], xs.at[i, c], xr.at[h, c],
-                device_id={"heads": peer}, device_id_type=MESH,
-            )
-            cp.start()
-            sends.append(cp)
+            pl.semaphore_wait(barrier, len(hp) + 1 + z * H)
+            greet(ready, False)
+
+        @pl.when(strand == FIRST)
+        def _():
+            for i in range(len(hp)):
+                x_copy(i, c).start()
 
     half = KDIM // 2
     step = -math.log(10000.0) / half
@@ -129,28 +150,49 @@
     qcos = jnp.cos(qang)
     qsin = jnp.where(qlane < half, -1.0, 1.0) * jnp.sin(qang)
 
-    loads[5].wait()
-    for i in range(0, D, 128):
-        wt[:, i : i + 128, :] = jnp.swapaxes(wraw[i : i + 128], 0, 1)
-
-    for peer in hp:
+    gate = max(NX - 2, 0)
+
+    @pl.when(strand == FIRST)
+    def _():
+        for i in range(len(hp)):
+            x_copy(i, gate).wait_send()
+        pl.semaphore_signal(turn, inc=1, device_id={"strand": other_strand}, device_id_type=MESH)
+
+    @pl.when(strand != FIRST)
+    def _():
+        pl.semaphore_wait(turn, 1)
         for c in range(NX):
-            pltpu.make_async_remote_copy(
-                xbuf.at[peer, c], xbuf.at[peer, c], xs.at[0, c], xr.at[peer, c],
-                device_id={"heads": peer}, device_id_type=MESH,
-            ).wait_recv()
-    loads[7].wait()
-    loads[8].wait()
-    loads[9].wait()
-    x = jnp.concatenate([xbuf[i, c] for i in range(H) for c in range(NX)], axis=1)
-    xf = x.astype(F32)
-    scale = lax.rsqrt(jnp.mean(xf * xf, axis=1, keepdims=True) + 1e-06)
-    normed = (xf * scale * spread(g1_ref[...], 0, D // 128)).astype(BF16)
-
-    loads[1].wait()
-    loads[2].wait()
-    kv_own = lax.dot_general(wkv[...], normed, NT, preferred_element_type=F32)
-    kvbuf[z, h] = kv_own.astype(BF16)
+            for i in range(len(hp)):
+                x_copy(i, c).start()
+
+
+    for k in (1, 2, 3, 7, 8, 9):
+        loads[k].wait()
+    kv_sum = jnp.zeros((kvl, rows), F32)
+    q_sum = jnp.zeros((rows, lh * KDIM), F32)
+    total_square = jnp.zeros((rows, 1), F32)
+    for peer in [h] + hp:
+        for c in range(NX):
+            if peer is not h:
+                pltpu.make_async_remote_copy(
+                    xbuf.at[peer, c], xbuf.at[peer, c], xs.at[0, c], xr.at[peer, c],
+                    device_id={"heads": peer}, device_id_type=MESH,
+                ).wait_recv()
+            piece = xbuf[peer, c].astype(F32)
+            total_square = total_square + jnp.sum(piece * piece, axis=1, keepdims=True)
+            first = peer * dl + c * xw
+            gain = jnp.concatenate(
+                [g1_ref[pl.ds(first // 128 + j, 1), :] for j in range(xw // 128)], axis=1
+            )
+            gained = (piece * gain).astype(BF16)
+            at = pl.ds(pl.multiple_of(first, 128), xw)
+            kv_sum = kv_sum + lax.dot_general(wkv[:, at], gained, NT, preferred_element_type=F32)
+            if peer is hp[-1] and c == NX - 1:
+                break
+            q_sum = q_sum + jnp.dot(gained, wq[at, :], preferred_element_type=F32)
+    scale = lax.rsqrt(total_square / D + 1e-06)
+    scale_row = jnp.transpose(jnp.broadcast_to(scale, (rows, 128)))[:1, :]
+    kvbuf[z, h] = (kv_sum * scale_row).astype(BF16)
 
     def kv_copy(p, hh, send, target):
         return pltpu.make_async_remote_copy(
@@ -158,32 +200,58 @@
             device_id=target, device_id_type=MESH,
         )
 
+    @pl.when(z < N - 1)
+    def _():
+        pl.semaphore_wait(ready, (N - 1 - z) * H)
+
     for i in range(N - 1):
-        cp = kv_copy(z, h, kvs.at[i], {"pos": farthest(z, i, N)})
+        p = farthest(z, i, N)
+        cp = kv_copy(z, h, kvs.at[i], {"pos": p})
         cp.start()
         sends.append(cp)
-    for i, peer in enumerate(hp):
-        cp = kv_copy(z, h, kfs.at[i, 0], {"heads": peer})
-        cp.start()
-        sends.append(cp)
-
-    loads[3].wait()
-    queries = jnp.dot(normed, wq[...], preferred_element_type=F32).astype(BF16).astype(F32)
+
+        @pl.when(direct(p))
+        def _():
+            for j, other in enumerate(hp):
+                kv_copy(z, h, kds.at[j, i], {"pos": p, "heads": other}).start()
+
+        if i > 0:
+            continue
+        for j, other in enumerate(hp):
+            cp = kv_copy(z, h, kfs.at[j, 0], {"heads": other})
+            cp.start()
+            sends.append(cp)
+
+    q_sum = q_sum + jnp.dot(gained, wq[at, :], preferred_element_type=F32)
+    queries = (q_sum * scale).astype(BF16).astype(F32)
     rotated = []
     for a in range(lh):
         qa = queries[:, a * KDIM : (a + 1) * KDIM]
         rotated.append((qa * qcos + pltpu.roll(qa, half, 1) * qsin).astype(BF16))
 
-    for j, peer in enumerate(zp):
-        kv_copy(peer, h, kvs.at[0], {"pos": peer}).wait_recv()
-        for i, other in enumerate(hp):
-            cp = kv_copy(peer, h, kfs.at[i, j + 1], {"heads": other})
-            cp.start()
-            sends.append(cp)
+    @pl.when(strand == FIRST)
+    def _():
+        for j, other in enumerate(hp):
+            kv_copy(z, other, kfs.at[j, 0], {"heads": other}).wait_recv()
+            for i, peer in enumerate(zp):
+                @pl.when(jnp.logical_not(direct(peer)))
+                def _():
+                    kv_copy(z, other, kfs.at[j, i + 1], {"pos": peer}).start()
+
+    loads[5].wait()
+    for i in range(0, D, 128):
+        wt[:, i : i + 128, :] = jnp.swapaxes(wraw[i : i + 128], 0, 1)
     score_parts, vts = [[] for _ in range(lh)], []
     for p in [z] + zp:
-        for other in hp:
-            kv_copy(p, other, kfs.at[0, 0], {"heads": other}).wait_recv()
+        if p is not z:
+            kv_copy(p, h, kvs.at[0], {"pos": p}).wait_recv()
+            for other in hp:
+                kv_copy(p, other, kfs.at[0, 0], {"heads": other}).wait_recv()
+        else:
+            @pl.when(strand != FIRST)
+            def _():
+                for other in hp:
+                    kv_copy(z, other, kfs.at[0, 0], {"heads": other}).wait_recv()
         kt = jnp.concatenate([kvbuf[p, i, :kl, :] for i in range(H)], axis=0).astype(F32)
         lo, hi = kt[:half], kt[half:]
         kt = jnp.concatenate(
@@ -195,6 +263,7 @@
                 jnp.dot(rotated[a], kt, preferred_element_type=F32) * KDIM ** (-0.5)
             )
     vt = jnp.concatenate(vts, axis=1)
+    x = jnp.concatenate([xbuf[i, c] for i in range(H) for c in range(NX)], axis=1)
     heads_out = []
     for a in range(lh):
         scores = jnp.concatenate(score_parts[a], axis=1)
@@ -218,7 +287,6 @@
             )
             cp.start()
             sends.append(cp)
-    other_strand = 1 - strand
     hr = rows // 2
     swaps = []
     square = jnp.zeros((rows, 1), F32)
@@ -261,6 +329,26 @@
         out_ref[other_strand, r * hr : (r + 1) * hr, :] = rcv[r]
     for cp in sends:
         cp.wait_send()
+    for i in range(len(hp)):
+        for c in range(NX):
+            if c != gate:
+                x_copy(i, c).wait_send()
+
+        @pl.when(strand != FIRST)
+        def _():
+            x_copy(i, gate).wait_send()
+
+        for j in range(N - 1):
+            p = farthest(z, j, N)
+
+            @pl.when(direct(p))
+            def _():
+                kv_copy(z, h, kds.at[i, j], {"pos": p, "heads": hp[i]}).wait_send()
+
+        for j, peer in enumerate(zp):
+            @pl.when(jnp.logical_not(direct(peer)))
+            def _():
+                kv_copy(z, hp[i], kfs.at[i, j + 1], {"pos": peer}).wait_send()
 
 
 def average(H, tracks_ref, tp_ref, out_ref):
@@ -324,10 +412,13 @@
             dma((zm,)),
             dma((N, H)),
             dma((hm, N)),
+            dma((hm, zm)),
             dma((hm, NC)),
             dma((H, NC)),
             dma((2,)),
             dma((2,)),
+            pltpu.SemaphoreType.REGULAR,
+            pltpu.SemaphoreType.REGULAR,
         ],
         compiler_params=pltpu.CompilerParams(
             collective_id=0, has_side_effects=True, vmem_limit_bytes=60 * 1024 * 1024

time: 30.2 us -> 28.4 us (0.940)
  Pallas kernels: 30 us -> 28.3 us
    pallas_call x1, Pallas kernels: 29.1 us -> 27.3 us  [body(): pl.pallas_call(functools.partial(kernel, H, N, NC, NX), out_shape=[pltpu....]
where the time goes in v1:
time: 28.4 us; the launch traced here: 28.3 us
  Pallas kernels  28.3 us (100%)
    pallas_call x1, Pallas kernels, body(): pl.pallas_call(functools.partial(kernel, H, N, NC, NX), out_shape=[pltpu....  27.3 us
    pallas_call x1, Pallas kernels, body(): pl.pallas_call(functools.partial(average, H), out_shape=jax.ShapeDtypeStr...  0.94 us

profile of v1, /device:TPU:0, one launch (start us, length us, event | category | flops | bytes accessed | tf_op | source)
XLA Modules:
  0.0 28.3 jit_solution(13202797979101040330)
XLA Ops:
  0.0 27.3 %shard_map.100 = (bf16[2,128,768]{2,1,0:T(8,128)(2,1)S(1)}, s32[6,128]{1,0:T(8,128)S(1)}) custom-call(s32[128,128]{1,0:T(8,128)} %bitcast.8, bf16[512,768]{1,0:T(8,128)(2,1)} %et_hbm.1, f32[12,128]{1,0:T(8,128)} %bitcast.9, bf16[1536,512]{1,0:T(8,128)(2,1)} %wq_hbm.1, bf16[64,1536]{1,0:T(8,128)(2,1)} %bitcast.7, bf16[96,1536]{1,0:T(8,128)(2,1)} %bitcast.6, ...), custom_call_target="tpu_custom_call" | custom-call | tf_op jit(solution)/shard_map/pallas_call | solution.py:384
  27.3 0.9 %shard_map.101 = f32[128,768]{1,0:T(8,128)} custom-call(bf16[2,128,768]{2,1,0:T(8,128)(2,1)S(1)} %get-tuple-element.7.tracks_ref, s32[6,128]{1,0:T(8,128)S(1)} %get-tuple-element.8.tp_ref), custom_call_target="tpu_custom_call" | custom-call | tf_op jit(solution)/shard_map/pallas_call | solution.py:439

commit v2 on v1

v2 whole, which is shorter than its diff:
```python
import functools
import math

import jax
import jax.numpy as jnp
from jax import lax
from jax.experimental import pallas as pl
from jax.experimental.pallas import tpu as pltpu
from jax.sharding import PartitionSpec as P

KDIM = 128
VDIM = 192
BIN = 128
F32 = jnp.float32
BF16 = jnp.bfloat16
MESH = pl.DeviceIdType.MESH
NT = (((1,), (1,)), ((), ()))
FIRST = 1
GROUPS = (2, 4, 4, 2)
PARTS = 4


def spread(table, first, count):
    return jnp.concatenate([table[first + i : first + i + 1, :] for i in range(count)], axis=1)


def partner(z, step, N):
    if N & (N - 1):
        return lax.rem(z + step, N)
    bit = 1
    while bit < N:
        if step & bit:
            z = z + bit - 2 * bit * ((z // bit) % 2)
        bit *= 2
    return z


def farthest(z, k, N):
    up = (N - 1 - z - k + N - 1) // N
    return up * (N - 1 - k) + (1 - up) * (k + z - (N - 1))


def kernel(
    H, N, NC, NX,
    codes_hbm, et_hbm, g1_hbm, wq_hbm, wk_hbm, wv_hbm, wo_hbm, g2_hbm, wt_hbm, tp_hbm,
    out_ref,
    tp_ref, codes_ref, gains, et, wq, wkv, wo, wraw, wt, xbuf, kvbuf, tabc, tabs, own, psend, precv, lg, snd, rcv,
    ls, xs, xr, kvs, kvr, ss, sr, ready, turn,
):
    h = lax.axis_index("heads")
    z = lax.axis_index("pos")
    strand = lax.axis_index("strand")
    rows = codes_hbm.shape[0]
    dl = et.shape[1]
    D = dl * H
    kl = wk_hbm.shape[0]
    kvl = wkv.shape[0]
    lh = wq.shape[1] // KDIM
    cols = wt.shape[2]
    total = rows * N

    hp = [lax.rem(h + i, H) for i in range(1, H)]
    zp = [partner(z, i, N) for i in range(1, N)]
    other_strand = 1 - strand

    def direct(p):
        return (4 * p < N) | (2 * (z - p) >= N)

    barrier = pltpu.get_barrier_semaphore()

    def greet(sem, up):
        for peer in zp:
            @pl.when(peer > z if up else peer < z)
            def _():
                for other in [h] + hp:
                    pl.semaphore_signal(
                        sem, inc=1, device_id={"pos": peer, "heads": other}, device_id_type=MESH
                    )

    greet(barrier, True)
    for peer in hp:
        pl.semaphore_signal(barrier, inc=1, device_id={"heads": peer}, device_id_type=MESH)
    pl.semaphore_signal(barrier, inc=1, device_id={"strand": other_strand}, device_id_type=MESH)

    xw = dl // NX
    load_codes = pltpu.make_async_copy(codes_hbm, codes_ref, ls.at[0])
    load_wq = pltpu.make_async_copy(wq_hbm, wq, ls.at[0])
    load_et = [
        pltpu.make_async_copy(
            et_hbm.at[:, pl.ds(c * xw, xw)], et.at[:, pl.ds(c * xw, xw)], ls.at[1 + c]
        )
        for c in range(NX)
    ]
    load_tp = pltpu.make_async_copy(tp_hbm, tp_ref, ls.at[1])
    load_wt = pltpu.make_async_copy(wt_hbm, wraw, ls.at[2])
    load_wo = pltpu.make_async_copy(wo_hbm, wo, ls.at[3])
    load_codes.start()
    for cp in load_et:
        cp.start()
    pltpu.make_async_copy(g1_hbm, gains.at[0], ls.at[1 + NX]).start()
    pltpu.make_async_copy(g2_hbm, gains.at[1], ls.at[1 + NX]).start()

    fwd = strand == 0
    width = 4 * BIN
    src_row = lax.broadcasted_iota(jnp.int32, (BIN, width), 0)
    place = lax.broadcasted_iota(jnp.int32, (BIN, width), 1) // 4
    want = jnp.where(fwd, place, BIN - 1 - place)
    expand = (src_row == want).astype(F32).astype(BF16)
    load_codes.wait()
    repeated = jnp.dot(codes_ref[...].astype(F32).astype(BF16), expand, preferred_element_type=F32)
    letter = lax.broadcasted_iota(jnp.int32, (rows, width), 1) % 4
    letter = jnp.where(fwd, letter, 3 - letter).astype(F32)
    onehot = (repeated == letter).astype(F32).astype(BF16)

    pltpu.make_async_copy(wk_hbm, wkv.at[pl.ds(0, kl), :], ls.at[2 + NX]).start()
    pltpu.make_async_copy(wv_hbm, wkv.at[pl.ds(kl, kvl - kl), :], ls.at[2 + NX]).start()
    load_wq.start()
    gate = max(NX - 2, 0)

    def x_copy(i, c):
        return pltpu.make_async_remote_copy(
            xbuf.at[h, c], xbuf.at[h, c], xs.at[int(c > gate)], xr.at[H - 2 - i, int(c > gate)],
            device_id={"heads": hp[i]}, device_id_type=MESH,
        )

    def x_wait(part, i, count, first):
        chunks = pl.ds(0, gate + 1) if part == 0 else pl.ds(gate + 1, NX - 1 - gate)
        ref = xbuf.at[pl.ds(first, count), chunks]
        return pltpu.make_async_remote_copy(
            ref, ref, xs.at[part], xr.at[i, part], device_id={"heads": hp[i]}, device_id_type=MESH
        )

    for c in range(NX):
        load_et[c].wait()
        part = jnp.dot(onehot, et[:, c * xw : (c + 1) * xw], preferred_element_type=F32)
        xbuf[h, c] = part.astype(BF16)
        if c == 0:
            pl.semaphore_wait(barrier, len(hp) + 1 + z * H)
            greet(ready, False)

        @pl.when(strand == FIRST)
        def _():
            for i in range(len(hp)):
                x_copy(i, c).start()
    load_wt.start()
    load_wo.start()
    load_tp.start()

    half = KDIM // 2
    step = -math.log(10000.0) / half
    lane_pos = lax.broadcasted_iota(jnp.int32, (half, rows), 1)
    kinv = jnp.exp(lax.broadcasted_iota(jnp.int32, (half, rows), 0).astype(F32) * step)
    for p in range(N):
        pos = lane_pos + p * rows
        pos = jnp.where(fwd, pos, total - 1 - pos).astype(F32)
        tabc[p] = jnp.cos(pos * kinv)
        tabs[p] = jnp.sin(pos * kinv)
    qpos = lax.broadcasted_iota(jnp.int32, (rows, KDIM), 0) + z * rows
    qpos = jnp.where(fwd, qpos, total - 1 - qpos).astype(F32)
    qlane = lax.broadcasted_iota(jnp.int32, (rows, KDIM), 1)
    qang = qpos * jnp.exp((qlane % half).astype(F32) * step)
    qcos = jnp.cos(qang)
    qsin = jnp.where(qlane < half, -1.0, 1.0) * jnp.sin(qang)


    @pl.when(strand == FIRST)
    def _():
        x_wait(0, 0, H - 1, 0).wait_send()
        pl.semaphore_signal(turn, inc=1, device_id={"strand": other_strand}, device_id_type=MESH)

    @pl.when(strand != FIRST)
    def _():
        pl.semaphore_wait(turn, 1)
        for c in range(NX):
            for i in range(len(hp)):
                x_copy(i, c).start()


    pltpu.make_async_copy(gains, gains, ls.at[1 + NX]).wait()
    pltpu.make_async_copy(wkv, wkv, ls.at[2 + NX]).wait()
    load_wq.wait()
    kv_sum = jnp.zeros((kvl, rows), F32)
    q_sum = jnp.zeros((rows, lh * KDIM), F32)
    total_square = jnp.zeros((rows, 1), F32)
    for k, peer in enumerate([h] + hp):
        for c in range(NX):
            if k > 0 and c in (0, gate + 1):
                x_wait(int(c > gate), k - 1, 1, peer).wait_recv()
            piece = xbuf[peer, c].astype(F32)
            total_square = total_square + jnp.sum(piece * piece, axis=1, keepdims=True)
            first = peer * dl + c * xw
            gain = jnp.concatenate(
                [gains[0, pl.ds(first // 128 + j, 1), :] for j in range(xw // 128)], axis=1
            )
            gained = (piece * gain).astype(BF16)
            at = pl.ds(pl.multiple_of(first, 128), xw)
            kv_sum = kv_sum + lax.dot_general(wkv[:, at], gained, NT, preferred_element_type=F32)
            if peer is hp[-1] and c == NX - 1:
                break
            q_sum = q_sum + jnp.dot(gained, wq[at, :], preferred_element_type=F32)
    scale = lax.rsqrt(total_square / D + 1e-06)
    scale_row = jnp.transpose(jnp.broadcast_to(scale, (rows, 128)))[:1, :]
    kvbuf[z, h] = (kv_sum * scale_row).astype(BF16)

    def kv_copy(p, hh, send, target):
        return pltpu.make_async_remote_copy(
            kvbuf.at[p, hh], kvbuf.at[p, hh], send, kvr.at[p],
            device_id=target, device_id_type=MESH,
        )

    def kv_wait(ref, send, p):
        return pltpu.make_async_remote_copy(
            ref, ref, send, kvr.at[p], device_id={"heads": hp[0]}, device_id_type=MESH
        )

    @pl.when(z < N - 1)
    def _():
        pl.semaphore_wait(ready, (N - 1 - z) * H)

    for j, other in enumerate(hp):
        kv_copy(z, h, ss, {"heads": other}).start()
    for i in range(N - 1):
        p = farthest(z, i, N)
        kv_copy(z, h, kvs, {"pos": p}).start()

        @pl.when(direct(p))
        def _():
            for j, other in enumerate(hp):
                kv_copy(z, h, kvs, {"pos": p, "heads": other}).start()

    q_sum = q_sum + jnp.dot(gained, wq[at, :], preferred_element_type=F32)
    queries = (q_sum * scale).astype(BF16).astype(F32)
    rotated = []
    for a in range(lh):
        qa = queries[:, a * KDIM : (a + 1) * KDIM]
        rotated.append((qa * qcos + pltpu.roll(qa, half, 1) * qsin).astype(BF16))

    kv_wait(kvbuf.at[z, pl.ds(0, H - 1)], ss, z).wait_recv()
    for peer in zp:
        @pl.when(jnp.logical_not(direct(peer)))
        def _():
            for other in hp:
                kv_copy(z, other, kvs, {"pos": peer}).start()

    load_wt.wait()
    for i in range(0, D, 128):
        wt[:, i : i + 128, :] = jnp.swapaxes(wraw[i : i + 128], 0, 1)
    score_parts, vts = [[] for _ in range(lh)], []
    for p in [z] + zp:
        if p is not z:
            kv_wait(kvbuf.at[p], kvs, p).wait_recv()
        kt = jnp.concatenate([kvbuf[p, i, :kl, :] for i in range(H)], axis=0).astype(F32)
        lo, hi = kt[:half], kt[half:]
        kt = jnp.concatenate(
            [lo * tabc[p] - hi * tabs[p], hi * tabc[p] + lo * tabs[p]], axis=0
        ).astype(BF16)
        vts.append(jnp.concatenate([kvbuf[p, i, kl:, :] for i in range(H)], axis=0))
        for a in range(lh):
            score_parts[a].append(
                jnp.dot(rotated[a], kt, preferred_element_type=F32) * KDIM ** (-0.5)
            )
    vt = jnp.concatenate(vts, axis=1)
    x = jnp.concatenate([xbuf[i, c] for i in range(H) for c in range(NX)], axis=1)
    heads_out = []
    for a in range(lh):
        scores = jnp.concatenate(score_parts[a], axis=1)
        top = jnp.max(scores, axis=1, keepdims=True)
        weights = jnp.exp(scores - top)
        weight_sum = jnp.sum(weights, axis=1, keepdims=True)
        mixed = lax.dot_general(weights.astype(BF16), vt, NT, preferred_element_type=F32)
        heads_out.append(mixed / weight_sum)
    merged = jnp.concatenate(heads_out, axis=1).astype(BF16)

    load_wo.wait()
    uw = D // sum(GROUPS)
    edges = [sum(GROUPS[:c]) for c in range(NC + 1)]

    def part_copy(c, i, owner, slot):
        units = pl.ds(edges[c], GROUPS[c])
        return pltpu.make_async_remote_copy(
            psend.at[units], precv.at[owner, units], xs.at[0], xr.at[slot, c],
            device_id={"heads": hp[i]}, device_id_type=MESH,
        )

    @pl.when(strand != FIRST)
    def _():
        x_wait(0, 0, H - 1, 0).wait_send()

    for c in range(NC):
        lo, hi = edges[c] * uw, edges[c + 1] * uw
        part = jnp.dot(merged, wo[:, lo:hi], preferred_element_type=F32)
        rounded = part.astype(BF16)
        for u in range(GROUPS[c]):
            psend[edges[c] + u] = rounded[:, u * uw : (u + 1) * uw]
        for i in range(len(hp)):
            part_copy(c, i, h, H - 2 - i).start()
        own[:, lo:hi] = x[:, lo:hi].astype(F32) + part
    x_wait(1, 0, H - 1, 0).wait_send()
    kv_wait(kvbuf.at[z, pl.ds(0, H - 1)], ss, z).wait_send()
    kv_wait(kvbuf.at[pl.ds(0, N - 1)], kvs, z).wait_send()
    load_tp.wait()
    hr = rows // 2
    swaps = []
    square = jnp.zeros((rows, 1), F32)
    blocks = cols // 128
    lane = lax.broadcasted_iota(jnp.int32, (1, 128), 1)
    stays = [
        tp_ref[b : b + 1, :] == (strand * H + h) * cols + b * 128 + lane for b in range(blocks)
    ]

    def cross(values, b, forward):
        swapped = jnp.where(lane % 2 == 0, pltpu.roll(values, 127, 1), pltpu.roll(values, 1, 1))
        return jnp.where(stays[b] | forward, values, swapped)

    for c in range(NC):
        a, e = edges[c] * uw, edges[c + 1] * uw
        summed = own[:, a:e]
        for i, peer in enumerate(hp):
            part_copy(c, i, peer, i).wait_recv()
            summed = summed + jnp.concatenate(
                [precv[peer, u].astype(F32) for u in range(edges[c], edges[c + 1])], axis=1
            )
        hidden = summed.astype(BF16).astype(F32)
        square = square + jnp.sum(hidden * hidden, axis=1, keepdims=True)
        gained = (hidden * spread(gains[1], a // 128, (e - a) // 128)).astype(BF16)
        last = c == NC - 1
        for s in (other_strand, strand):
            part = jnp.dot(gained, wt[s, a:e, :], preferred_element_type=F32)
            if c > 0:
                part = lg[s] + part
            if not last:
                lg[s] = part
                continue
            logits = part * lax.rsqrt(square / D + 1e-06)
            for r in range(2):
                part = logits[r * hr : (r + 1) * hr]
                track = (jnp.maximum(part, 0.0) + jnp.log1p(jnp.exp(-jnp.abs(part)))).astype(BF16)
                if s is strand:
                    for b in range(blocks):
                        at = slice(b * 128, (b + 1) * 128)
                        out_ref[r * hr : (r + 1) * hr, at] = 0.5 * cross(
                            track[:, at].astype(F32), b, fwd
                        )
                    continue
                snd[r] = track
                cp = pltpu.make_async_remote_copy(
                    snd.at[r], rcv.at[r], ss, sr.at[r],
                    device_id={"strand": other_strand}, device_id_type=MESH,
                )
                cp.start()
                swaps.append(cp)
    sent = precv.at[pl.ds(0, H - 1)]
    pltpu.make_async_remote_copy(
        sent, sent, xs.at[0], xr.at[0, 0], device_id={"heads": hp[0]}, device_id_type=MESH
    ).wait_send()
    for r in range(2):
        swaps[r].wait_recv()
        for b in range(blocks):
            at = slice(b * 128, (b + 1) * 128)
            rr = slice(r * hr, (r + 1) * hr)
            out_ref[rr, at] = out_ref[rr, at] + 0.5 * cross(
                rcv[r, :, at].astype(F32), b, jnp.logical_not(fwd)
            )
    pltpu.make_async_remote_copy(
        snd, rcv, ss, sr.at[0], device_id={"strand": other_strand}, device_id_type=MESH
    ).wait_send()


def store(src_ref, out_ref, sem):
    rows = src_ref.shape[0]
    step = rows // PARTS
    copies = [
        pltpu.make_async_copy(
            src_ref.at[pl.ds(i * step, step)], out_ref.at[pl.ds(i * step, step)], sem.at[i]
        )
        for i in range(PARTS)
    ]
    for cp in copies:
        cp.start()
    for cp in copies:
        cp.wait()


def body(
    base_codes, embed_table, attn_gain, w_query, w_key, w_value, w_out, head_gain, w_tracks, track_pairs
):
    H = lax.axis_size("heads")
    N = lax.axis_size("pos")
    rows = base_codes.shape[0] // BIN
    dl = embed_table.shape[1]
    D = dl * H
    cols = w_tracks.shape[2]
    kvl = w_key.shape[1] + w_value.shape[1]
    NC, NX = len(GROUPS), 3
    vm = pl.BlockSpec(memory_space=pltpu.VMEM)
    hbm = pl.BlockSpec(memory_space=pl.ANY)
    dma = pltpu.SemaphoreType.DMA
    hm = max(H - 1, 1)
    tracks = pl.pallas_call(
        functools.partial(kernel, H, N, NC, NX),
        out_shape=pltpu.VMEM((rows, cols), F32),
        in_specs=[hbm] * 10,
        out_specs=vm,
        scratch_shapes=[
            pltpu.VMEM((cols // 128, 128), jnp.int32),
            pltpu.VMEM((rows, BIN), jnp.int32),
            pltpu.VMEM((2, D // 128, 128), F32),
            pltpu.VMEM(embed_table.shape, BF16),
            pltpu.VMEM(w_query.shape, BF16),
            pltpu.VMEM((kvl, D), BF16),
            pltpu.VMEM(w_out.shape, BF16),
            pltpu.VMEM(w_tracks.shape, BF16),
            pltpu.VMEM((2, D, cols), BF16),
            pltpu.VMEM((H, NX, rows, dl // NX), BF16),
            pltpu.VMEM((N, H, kvl, rows), BF16),
            pltpu.VMEM((N, KDIM // 2, rows), F32),
            pltpu.VMEM((N, KDIM // 2, rows), F32),
            pltpu.VMEM((rows, D), F32),
            pltpu.VMEM((sum(GROUPS), rows, D // sum(GROUPS)), BF16),
            pltpu.VMEM((H, sum(GROUPS), rows, D // sum(GROUPS)), BF16),
            pltpu.VMEM((2, rows, cols), F32),
            pltpu.VMEM((2, rows // 2, cols), BF16),
            pltpu.VMEM((2, rows // 2, cols), BF16),
            dma((3 + NX,)),
            dma((2,)),
            dma((hm, NC)),
            dma,
            dma((N,)),
            dma,
            dma((2,)),
            pltpu.SemaphoreType.REGULAR,
            pltpu.SemaphoreType.REGULAR,
        ],
        compiler_params=pltpu.CompilerParams(
            collective_id=0, has_side_effects=True, vmem_limit_bytes=60 * 1024 * 1024
        ),
    )(
        base_codes.reshape(rows, BIN),
        embed_table,
        attn_gain.reshape(D // 128, 128),
        w_query,
        w_key.T,
        w_value.T,
        w_out,
        head_gain.reshape(D // 128, 128),
        w_tracks,
        track_pairs.reshape(cols // 128, 128),
    )
    return tracks


def solution(mesh):
    placed = (
        P(("groups", "pos")),
        P(None, "heads"),
        P(),
        P(None, "heads"),
        P(None, "heads"),
        P(None, "heads"),
        P("heads", None),
        P(),
        P(None, None, "heads"),
        P(("strand", "heads")),
    )
    return jax.shard_map(
        body,
        mesh=mesh,
        in_specs=placed,
        out_specs=P(("groups", "pos"), ("strand", "heads")),
        check_vma=False,
    )
```

time: 28.4 us -> 27.3 us (0.961)
  Pallas kernels: 28.3 us -> 26.4 us
  local copies, waits for them, and re-layouts: 0 us -> 0.75 us
    pallas_call x2 -> x1, Pallas kernels: 28.3 us -> 26.4 us  [body(): pl.pallas_call(functools.partial(kernel, H, N, NC, NX), out_shape=pltpu.V...]
    unnamed x0 -> x1, local copies, waits for them, and re-layouts: none -> 0.75 us
where the time goes in v2:
time: 27.3 us; the launch traced here: 27.1 us
  Pallas kernels  26.4 us (97%)
  local copies, waits for them, and re-layouts  0.75 us (3%)
    pallas_call x1, Pallas kernels, body(): pl.pallas_call(functools.partial(kernel, H, N, NC, NX), out_shape=pltpu.V...  26.4 us
    unnamed x1, local copies, waits for them, and re-layouts  0.75 us

profile of v2, /device:TPU:0, one launch (start us, length us, event | category | flops | bytes accessed | tf_op | source)
XLA Modules:
  0.0 27.1 jit_solution(9055351518907792973)
XLA Ops:
  0.0 26.4 %shard_map.100 = f32[128,768]{1,0:T(8,128)S(1)} custom-call(s32[128,128]{1,0:T(8,128)} %bitcast.8, bf16[512,768]{1,0:T(8,128)(2,1)} %et_hbm.1, f32[12,128]{1,0:T(8,128)} %bitcast.9, bf16[1536,512]{1,0:T(8,128)(2,1)} %wq_hbm.1, bf16[64,1536]{1,0:T(8,128)(2,1)} %bitcast.7, bf16[96,1536]{1,0:T(8,128)(2,1)} %bitcast.6, bf16[768,1536]{1,0:T(8,128)(2,1)} %wo_hbm.1, ...), custom_call_target="tpu_custom_call" | custom-call | tf_op jit(solution)/shard_map/pallas_call | solution.py:399
  26.4 0.7 %copy.12 = f32[128,768]{1,0:T(8,128)} copy(f32[128,768]{1,0:T(8,128)S(1)} %shard_map.100) | data formatting | bytes 786432

commit v3 on v2

--- a/solution.py
+++ b/solution.py
@@ -16,7 +16,7 @@
 MESH = pl.DeviceIdType.MESH
 NT = (((1,), (1,)), ((), ()))
 FIRST = 1
-GROUPS = (2, 4, 4, 2)
+GROUPS = (2, 3, 3, 2, 2)
 PARTS = 4
 
 
@@ -44,8 +44,8 @@
     H, N, NC, NX,
     codes_hbm, et_hbm, g1_hbm, wq_hbm, wk_hbm, wv_hbm, wo_hbm, g2_hbm, wt_hbm, tp_hbm,
     out_ref,
-    tp_ref, codes_ref, gains, et, wq, wkv, wo, wraw, wt, xbuf, kvbuf, tabc, tabs, own, psend, precv, lg, snd, rcv,
-    ls, xs, xr, kvs, kvr, ss, sr, ready, turn,
+    tp_ref, codes_ref, gains, et, wq, wkv, wo, wraw, wt, xbuf, kbuf, vbuf, tabc, tabs, own, psend, precv, lg, snd, rcv,
+    ls, xs, xr, ks, vs, kr, vr, ss, sr, ready, turn,
 ):
     h = lax.axis_index("heads")
     z = lax.axis_index("pos")
@@ -184,6 +184,12 @@
     total_square = jnp.zeros((rows, 1), F32)
     for k, peer in enumerate([h] + hp):
         for c in range(NX):
+            if k == 1 and c == 0:
+                @pl.when(strand != FIRST)
+                def _():
+                    x_wait(0, 0, H - 1, 0).wait_send()
+
+                x_wait(1, 0, H - 1, 0).wait_send()
             if k > 0 and c in (0, gate + 1):
                 x_wait(int(c > gate), k - 1, 1, peer).wait_recv()
             piece = xbuf[peer, c].astype(F32)
@@ -200,33 +206,39 @@
             q_sum = q_sum + jnp.dot(gained, wq[at, :], preferred_element_type=F32)
     scale = lax.rsqrt(total_square / D + 1e-06)
     scale_row = jnp.transpose(jnp.broadcast_to(scale, (rows, 128)))[:1, :]
-    kvbuf[z, h] = (kv_sum * scale_row).astype(BF16)
-
-    def kv_copy(p, hh, send, target):
+    kv_own = (kv_sum * scale_row).astype(BF16)
+    kbuf[z, h] = kv_own[:kl]
+    vbuf[z, h] = kv_own[kl:]
+    parts = ((kbuf, ks, kr, xs.at[0]), (vbuf, vs, vr, xs.at[1]))
+
+    def kv_copy(part, p, hh, send, target):
+        buf, _, recv, _ = part
         return pltpu.make_async_remote_copy(
-            kvbuf.at[p, hh], kvbuf.at[p, hh], send, kvr.at[p],
-            device_id=target, device_id_type=MESH,
-        )
-
-    def kv_wait(ref, send, p):
+            buf.at[p, hh], buf.at[p, hh], send, recv.at[p], device_id=target, device_id_type=MESH
+        )
+
+    def kv_wait(part, ref, send, p):
         return pltpu.make_async_remote_copy(
-            ref, ref, send, kvr.at[p], device_id={"heads": hp[0]}, device_id_type=MESH
+            ref, ref, send, part[2].at[p], device_id={"heads": hp[0]}, device_id_type=MESH
         )
 
     @pl.when(z < N - 1)
     def _():
         pl.semaphore_wait(ready, (N - 1 - z) * H)
 
-    for j, other in enumerate(hp):
-        kv_copy(z, h, ss, {"heads": other}).start()
     for i in range(N - 1):
         p = farthest(z, i, N)
-        kv_copy(z, h, kvs, {"pos": p}).start()
-
-        @pl.when(direct(p))
-        def _():
-            for j, other in enumerate(hp):
-                kv_copy(z, h, kvs, {"pos": p, "heads": other}).start()
+        for part in parts:
+            kv_copy(part, z, h, part[1], {"pos": p}).start()
+
+            @pl.when(direct(p))
+            def _():
+                for other in hp:
+                    kv_copy(part, z, h, part[1], {"pos": p, "heads": other}).start()
+
+            if i == 0:
+                for other in hp:
+                    kv_copy(part, z, h, part[3], {"heads": other}).start()
 
     q_sum = q_sum + jnp.dot(gained, wq[at, :], preferred_element_type=F32)
     queries = (q_sum * scale).astype(BF16).astype(F32)
@@ -235,12 +247,13 @@
         qa = queries[:, a * KDIM : (a + 1) * KDIM]
         rotated.append((qa * qcos + pltpu.roll(qa, half, 1) * qsin).astype(BF16))
 
-    kv_wait(kvbuf.at[z, pl.ds(0, H - 1)], ss, z).wait_recv()
-    for peer in zp:
-        @pl.when(jnp.logical_not(direct(peer)))
-        def _():
-            for other in hp:
-                kv_copy(z, other, kvs, {"pos": peer}).start()
+    for part in parts:
+        kv_wait(part, part[0].at[z, pl.ds(0, H - 1)], part[3], z).wait_recv()
+        for peer in zp:
+            @pl.when(jnp.logical_not(direct(peer)))
+            def _():
+                for other in hp:
+                    kv_copy(part, z, other, part[1], {"pos": peer}).start()
 
     load_wt.wait()
     for i in range(0, D, 128):
@@ -248,17 +261,20 @@
     score_parts, vts = [[] for _ in range(lh)], []
     for p in [z] + zp:
         if p is not z:
-            kv_wait(kvbuf.at[p], kvs, p).wait_recv()
-        kt = jnp.concatenate([kvbuf[p, i, :kl, :] for i in range(H)], axis=0).astype(F32)
+            kv_wait(parts[0], kbuf.at[p], ks, p).wait_recv()
+        kt = jnp.concatenate([kbuf[p, i] for i in range(H)], axis=0).astype(F32)
         lo, hi = kt[:half], kt[half:]
         kt = jnp.concatenate(
             [lo * tabc[p] - hi * tabs[p], hi * tabc[p] + lo * tabs[p]], axis=0
         ).astype(BF16)
-        vts.append(jnp.concatenate([kvbuf[p, i, kl:, :] for i in range(H)], axis=0))
         for a in range(lh):
             score_parts[a].append(
                 jnp.dot(rotated[a], kt, preferred_element_type=F32) * KDIM ** (-0.5)
             )
+    for p in [z] + zp:
+        if p is not z:
+            kv_wait(parts[1], vbuf.at[p], vs, p).wait_recv()
+        vts.append(jnp.concatenate([vbuf[p, i] for i in range(H)], axis=0))
     vt = jnp.concatenate(vts, axis=1)
     x = jnp.concatenate([xbuf[i, c] for i in range(H) for c in range(NX)], axis=1)
     heads_out = []
@@ -282,10 +298,7 @@
             device_id={"heads": hp[i]}, device_id_type=MESH,
         )
 
-    @pl.when(strand != FIRST)
-    def _():
-        x_wait(0, 0, H - 1, 0).wait_send()
-
+    kv_wait(parts[0], kbuf.at[z, pl.ds(0, H - 1)], xs.at[0], z).wait_send()
     for c in range(NC):
         lo, hi = edges[c] * uw, edges[c + 1] * uw
         part = jnp.dot(merged, wo[:, lo:hi], preferred_element_type=F32)
@@ -295,9 +308,9 @@
         for i in range(len(hp)):
             part_copy(c, i, h, H - 2 - i).start()
         own[:, lo:hi] = x[:, lo:hi].astype(F32) + part
-    x_wait(1, 0, H - 1, 0).wait_send()
-    kv_wait(kvbuf.at[z, pl.ds(0, H - 1)], ss, z).wait_send()
-    kv_wait(kvbuf.at[pl.ds(0, N - 1)], kvs, z).wait_send()
+    kv_wait(parts[1], vbuf.at[z, pl.ds(0, H - 1)], xs.at[1], z).wait_send()
+    for part in parts:
+        kv_wait(part, part[0].at[pl.ds(0, N - 1)], part[1], z).wait_send()
     load_tp.wait()
     hr = rows // 2
     swaps = []
@@ -412,7 +425,8 @@
             pltpu.VMEM(w_tracks.shape, BF16),
             pltpu.VMEM((2, D, cols), BF16),
             pltpu.VMEM((H, NX, rows, dl // NX), BF16),
-            pltpu.VMEM((N, H, kvl, rows), BF16),
+            pltpu.VMEM((N, H, w_key.shape[1], rows), BF16),
+            pltpu.VMEM((N, H, w_value.shape[1], rows), BF16),
             pltpu.VMEM((N, KDIM // 2, rows), F32),
             pltpu.VMEM((N, KDIM // 2, rows), F32),
             pltpu.VMEM((rows, D), F32),
@@ -425,6 +439,8 @@
             dma((2,)),
             dma((hm, NC)),
             dma,
+            dma,
+            dma((N,)),
             dma((N,)),
             dma,
             dma((2,)),

time: 27.3 us -> 27 us (0.989)
  Pallas kernels: 26.4 us -> 26.1 us
where the time goes in v3:
time: 27 us; the launch traced here: 26.9 us
  Pallas kernels  26.1 us (97%)
  local copies, waits for them, and re-layouts  0.75 us (3%)
    pallas_call x1, Pallas kernels, body(): pl.pallas_call(functools.partial(kernel, H, N, NC, NX), out_shape=pltpu.V...  26.1 us
    unnamed x1, local copies, waits for them, and re-layouts  0.75 us

profile of v3, /device:TPU:0, one launch (start us, length us, event | category | flops | bytes accessed | tf_op | source)
XLA Modules:
  0.0 26.9 jit_solution(1678020912371606886)
XLA Ops:
  0.0 26.1 %shard_map.100 = f32[128,768]{1,0:T(8,128)S(1)} custom-call(s32[128,128]{1,0:T(8,128)} %bitcast.8, bf16[512,768]{1,0:T(8,128)(2,1)} %et_hbm.1, f32[12,128]{1,0:T(8,128)} %bitcast.9, bf16[1536,512]{1,0:T(8,128)(2,1)} %wq_hbm.1, bf16[64,1536]{1,0:T(8,128)(2,1)} %bitcast.7, bf16[96,1536]{1,0:T(8,128)(2,1)} %bitcast.6, bf16[768,1536]{1,0:T(8,128)(2,1)} %wo_hbm.1, ...), custom_call_target="tpu_custom_call" | custom-call | tf_op jit(solution)/shard_map/pallas_call | solution.py:412
  26.1 0.7 %copy.12 = f32[128,768]{1,0:T(8,128)} copy(f32[128,768]{1,0:T(8,128)S(1)} %shard_map.100) | data formatting | bytes 786432

commit v4 on v3

--- a/solution.py
+++ b/solution.py
@@ -64,7 +64,7 @@
     other_strand = 1 - strand
 
     def direct(p):
-        return (4 * p < N) | (2 * (z - p) >= N)
+        return (4 * p < N) | (2 * (z - p) >= N) | ((strand == FIRST) & (z - p == 1))
 
     barrier = pltpu.get_barrier_semaphore()
 
@@ -82,12 +82,18 @@
         pl.semaphore_signal(barrier, inc=1, device_id={"heads": peer}, device_id_type=MESH)
     pl.semaphore_signal(barrier, inc=1, device_id={"strand": other_strand}, device_id_type=MESH)
 
-    xw = dl // NX
+    xunits = dl // 128
+    lead = max(1, xunits // 3)
+    after = max(1, xunits // 6)
+    xsizes = (lead, after, xunits - lead - after)
+    xat = [sum(xsizes[:c]) for c in range(NX + 1)]
     load_codes = pltpu.make_async_copy(codes_hbm, codes_ref, ls.at[0])
     load_wq = pltpu.make_async_copy(wq_hbm, wq, ls.at[0])
     load_et = [
         pltpu.make_async_copy(
-            et_hbm.at[:, pl.ds(c * xw, xw)], et.at[:, pl.ds(c * xw, xw)], ls.at[1 + c]
+            et_hbm.at[:, pl.ds(xat[c] * 128, xsizes[c] * 128)],
+            et.at[:, pl.ds(xat[c] * 128, xsizes[c] * 128)],
+            ls.at[1 + c],
         )
         for c in range(NX)
     ]
@@ -118,22 +124,26 @@
     gate = max(NX - 2, 0)
 
     def x_copy(i, c):
+        ref = xbuf.at[h, pl.ds(xat[c], xsizes[c])]
         return pltpu.make_async_remote_copy(
-            xbuf.at[h, c], xbuf.at[h, c], xs.at[int(c > gate)], xr.at[H - 2 - i, int(c > gate)],
+            ref, ref, xs.at[int(c > gate)], xr.at[H - 2 - i, int(c > gate)],
             device_id={"heads": hp[i]}, device_id_type=MESH,
         )
 
     def x_wait(part, i, count, first):
-        chunks = pl.ds(0, gate + 1) if part == 0 else pl.ds(gate + 1, NX - 1 - gate)
-        ref = xbuf.at[pl.ds(first, count), chunks]
+        units = pl.ds(0, xat[gate + 1]) if part == 0 else pl.ds(xat[gate + 1], xat[NX] - xat[gate + 1])
+        ref = xbuf.at[pl.ds(first, count), units]
         return pltpu.make_async_remote_copy(
             ref, ref, xs.at[part], xr.at[i, part], device_id={"heads": hp[i]}, device_id_type=MESH
         )
 
     for c in range(NX):
         load_et[c].wait()
-        part = jnp.dot(onehot, et[:, c * xw : (c + 1) * xw], preferred_element_type=F32)
-        xbuf[h, c] = part.astype(BF16)
+        part = jnp.dot(
+            onehot, et[:, xat[c] * 128 : xat[c + 1] * 128], preferred_element_type=F32
+        ).astype(BF16)
+        for u in range(xsizes[c]):
+            xbuf[h, xat[c] + u] = part[:, u * 128 : (u + 1) * 128]
         if c == 0:
             pl.semaphore_wait(barrier, len(hp) + 1 + z * H)
             greet(ready, False)
@@ -192,14 +202,16 @@
                 x_wait(1, 0, H - 1, 0).wait_send()
             if k > 0 and c in (0, gate + 1):
                 x_wait(int(c > gate), k - 1, 1, peer).wait_recv()
-            piece = xbuf[peer, c].astype(F32)
+            piece = jnp.concatenate(
+                [xbuf[peer, u].astype(F32) for u in range(xat[c], xat[c + 1])], axis=1
+            )
             total_square = total_square + jnp.sum(piece * piece, axis=1, keepdims=True)
-            first = peer * dl + c * xw
+            first = peer * dl + xat[c] * 128
             gain = jnp.concatenate(
-                [gains[0, pl.ds(first // 128 + j, 1), :] for j in range(xw // 128)], axis=1
+                [gains[0, pl.ds(first // 128 + j, 1), :] for j in range(xsizes[c])], axis=1
             )
             gained = (piece * gain).astype(BF16)
-            at = pl.ds(pl.multiple_of(first, 128), xw)
+            at = pl.ds(pl.multiple_of(first, 128), xsizes[c] * 128)
             kv_sum = kv_sum + lax.dot_general(wkv[:, at], gained, NT, preferred_element_type=F32)
             if peer is hp[-1] and c == NX - 1:
                 break
@@ -228,14 +240,15 @@
 
     for i in range(N - 1):
         p = farthest(z, i, N)
+
+        @pl.when(direct(p))
+        def _():
+            for part in parts:
+                for other in hp:
+                    kv_copy(part, z, h, part[1], {"pos": p, "heads": other}).start()
+
         for part in parts:
             kv_copy(part, z, h, part[1], {"pos": p}).start()
-
-            @pl.when(direct(p))
-            def _():
-                for other in hp:
-                    kv_copy(part, z, h, part[1], {"pos": p, "heads": other}).start()
-
             if i == 0:
                 for other in hp:
                     kv_copy(part, z, h, part[3], {"heads": other}).start()
@@ -276,7 +289,7 @@
             kv_wait(parts[1], vbuf.at[p], vs, p).wait_recv()
         vts.append(jnp.concatenate([vbuf[p, i] for i in range(H)], axis=0))
     vt = jnp.concatenate(vts, axis=1)
-    x = jnp.concatenate([xbuf[i, c] for i in range(H) for c in range(NX)], axis=1)
+    x = jnp.concatenate([xbuf[i, u] for i in range(H) for u in range(xunits)], axis=1)
     heads_out = []
     for a in range(lh):
         scores = jnp.concatenate(score_parts[a], axis=1)
@@ -424,7 +437,7 @@
             pltpu.VMEM(w_out.shape, BF16),
             pltpu.VMEM(w_tracks.shape, BF16),
             pltpu.VMEM((2, D, cols), BF16),
-            pltpu.VMEM((H, NX, rows, dl // NX), BF16),
+            pltpu.VMEM((H, dl // 128, rows, 128), BF16),
             pltpu.VMEM((N, H, w_key.shape[1], rows), BF16),
             pltpu.VMEM((N, H, w_value.shape[1], rows), BF16),
             pltpu.VMEM((N, KDIM // 2, rows), F32),

time: 27 us -> 26.4 us (0.978)
  Pallas kernels: 26.1 us -> 25.4 us
    pallas_call x1, Pallas kernels: 26.1 us -> 25.4 us  [body(): pl.pallas_call(functools.partial(kernel, H, N, NC, NX), out_shape=pltpu.V...]
where the time goes in v4:
time: 26.4 us; the launch traced here: 26.2 us
  Pallas kernels  25.4 us (96%)
  local copies, waits for them, and re-layouts  0.75 us (3%)
    pallas_call x1, Pallas kernels, body(): pl.pallas_call(functools.partial(kernel, H, N, NC, NX), out_shape=pltpu.V...  25.4 us
    unnamed x1, local copies, waits for them, and re-layouts  0.75 us

profile of v4, /device:TPU:0, one launch (start us, length us, event | category | flops | bytes accessed | tf_op | source)
XLA Modules:
  0.0 26.2 jit_solution(8354995746683199732)
XLA Ops:
  0.0 25.4 %shard_map.100 = f32[128,768]{1,0:T(8,128)S(1)} custom-call(s32[128,128]{1,0:T(8,128)} %bitcast.8, bf16[512,768]{1,0:T(8,128)(2,1)} %et_hbm.1, f32[12,128]{1,0:T(8,128)} %bitcast.9, bf16[1536,512]{1,0:T(8,128)(2,1)} %wq_hbm.1, bf16[64,1536]{1,0:T(8,128)(2,1)} %bitcast.7, bf16[96,1536]{1,0:T(8,128)(2,1)} %bitcast.6, bf16[768,1536]{1,0:T(8,128)(2,1)} %wo_hbm.1, ...), custom_call_target="tpu_custom_call" | custom-call | tf_op jit(solution)/shard_map/pallas_call | solution.py:425
  25.4 0.7 %copy.12 = f32[128,768]{1,0:T(8,128)} copy(f32[128,768]{1,0:T(8,128)S(1)} %shard_map.100) | data formatting | bytes 786432

commit v5 on v4

--- a/solution.py
+++ b/solution.py
@@ -17,7 +17,6 @@
 NT = (((1,), (1,)), ((), ()))
 FIRST = 1
 GROUPS = (2, 3, 3, 2, 2)
-PARTS = 4
 
 
 def spread(table, first, count):
@@ -33,11 +32,6 @@
             z = z + bit - 2 * bit * ((z // bit) % 2)
         bit *= 2
     return z
-
-
-def farthest(z, k, N):
-    up = (N - 1 - z - k + N - 1) // N
-    return up * (N - 1 - k) + (1 - up) * (k + z - (N - 1))
 
 
 def kernel(
@@ -239,7 +233,7 @@
         pl.semaphore_wait(ready, (N - 1 - z) * H)
 
     for i in range(N - 1):
-        p = farthest(z, i, N)
+        p = jnp.where(z <= i, i + 1, i)
 
         @pl.when(direct(p))
         def _():
@@ -262,7 +256,9 @@
 
     for part in parts:
         kv_wait(part, part[0].at[z, pl.ds(0, H - 1)], part[3], z).wait_recv()
-        for peer in zp:
+        for i in range(N - 1):
+            peer = jnp.where(z <= i, i + 1, i)
+
             @pl.when(jnp.logical_not(direct(peer)))
             def _():
                 for other in hp:
@@ -390,21 +386,6 @@
     pltpu.make_async_remote_copy(
         snd, rcv, ss, sr.at[0], device_id={"strand": other_strand}, device_id_type=MESH
     ).wait_send()
-
-
-def store(src_ref, out_ref, sem):
-    rows = src_ref.shape[0]
-    step = rows // PARTS
-    copies = [
-        pltpu.make_async_copy(
-            src_ref.at[pl.ds(i * step, step)], out_ref.at[pl.ds(i * step, step)], sem.at[i]
-        )
-        for i in range(PARTS)
-    ]
-    for cp in copies:
-        cp.start()
-    for cp in copies:
-        cp.wait()
 
 
 def body(

time: 26.4 us -> 26.3 us (level)
  no operation moved by 1% of the time
where the time goes in v5:
time: 26.3 us; the launch traced here: 26.2 us
  Pallas kernels  25.4 us (97%)
  local copies, waits for them, and re-layouts  0.75 us (3%)
    pallas_call x1, Pallas kernels, body(): pl.pallas_call(functools.partial(kernel, H, N, NC, NX), out_shape=pltpu.V...  25.4 us
    unnamed x1, local copies, waits for them, and re-layouts  0.75 us

profile of v5, /device:TPU:0, one launch (start us, length us, event | category | flops | bytes accessed | tf_op | source)
XLA Modules:
  0.0 26.2 jit_solution(974231405003630114)
XLA Ops:
  0.0 25.4 %shard_map.100 = f32[128,768]{1,0:T(8,128)S(1)} custom-call(s32[128,128]{1,0:T(8,128)} %bitcast.8, bf16[512,768]{1,0:T(8,128)(2,1)} %et_hbm.1, f32[12,128]{1,0:T(8,128)} %bitcast.9, bf16[1536,512]{1,0:T(8,128)(2,1)} %wq_hbm.1, bf16[64,1536]{1,0:T(8,128)(2,1)} %bitcast.7, bf16[96,1536]{1,0:T(8,128)(2,1)} %bitcast.6, bf16[768,1536]{1,0:T(8,128)(2,1)} %wo_hbm.1, ...), custom_call_target="tpu_custom_call" | custom-call | tf_op jit(solution)/shard_map/pallas_call | solution.py:406
  25.4 0.7 %copy.12 = f32[128,768]{1,0:T(8,128)} copy(f32[128,768]{1,0:T(8,128)S(1)} %shard_map.100) | data formatting | bytes 786432

commit v6 on v5

--- a/solution.py
+++ b/solution.py
@@ -79,7 +79,8 @@
     xunits = dl // 128
     lead = max(1, xunits // 3)
     after = max(1, xunits // 6)
-    xsizes = (lead, after, xunits - lead - after)
+    rest = xunits - lead - after
+    xsizes = (lead, after, rest - 1, 1) if NX > 3 else (lead, after, rest)
     xat = [sum(xsizes[:c]) for c in range(NX + 1)]
     load_codes = pltpu.make_async_copy(codes_hbm, codes_ref, ls.at[0])
     load_wq = pltpu.make_async_copy(wq_hbm, wq, ls.at[0])
@@ -115,20 +116,19 @@
     pltpu.make_async_copy(wk_hbm, wkv.at[pl.ds(0, kl), :], ls.at[2 + NX]).start()
     pltpu.make_async_copy(wv_hbm, wkv.at[pl.ds(kl, kvl - kl), :], ls.at[2 + NX]).start()
     load_wq.start()
-    gate = max(NX - 2, 0)
+    gate = 1
 
     def x_copy(i, c):
         ref = xbuf.at[h, pl.ds(xat[c], xsizes[c])]
         return pltpu.make_async_remote_copy(
-            ref, ref, xs.at[int(c > gate)], xr.at[H - 2 - i, int(c > gate)],
+            ref, ref, xs.at[int(c > gate)], xr.at[H - 2 - i, max(c - gate, 0)],
             device_id={"heads": hp[i]}, device_id_type=MESH,
         )
 
-    def x_wait(part, i, count, first):
-        units = pl.ds(0, xat[gate + 1]) if part == 0 else pl.ds(xat[gate + 1], xat[NX] - xat[gate + 1])
-        ref = xbuf.at[pl.ds(first, count), units]
+    def x_wait(part, i, count, first, start, end):
+        ref = xbuf.at[pl.ds(first, count), pl.ds(xat[start], xat[end] - xat[start])]
         return pltpu.make_async_remote_copy(
-            ref, ref, xs.at[part], xr.at[i, part], device_id={"heads": hp[i]}, device_id_type=MESH
+            ref, ref, xs.at[min(part, 1)], xr.at[i, part], device_id={"heads": hp[i]}, device_id_type=MESH
         )
 
     for c in range(NX):
@@ -169,7 +169,7 @@
 
     @pl.when(strand == FIRST)
     def _():
-        x_wait(0, 0, H - 1, 0).wait_send()
+        x_wait(0, 0, H - 1, 0, 0, gate + 1).wait_send()
         pl.semaphore_signal(turn, inc=1, device_id={"strand": other_strand}, device_id_type=MESH)
 
     @pl.when(strand != FIRST)
@@ -191,11 +191,13 @@
             if k == 1 and c == 0:
                 @pl.when(strand != FIRST)
                 def _():
-                    x_wait(0, 0, H - 1, 0).wait_send()
-
-                x_wait(1, 0, H - 1, 0).wait_send()
-            if k > 0 and c in (0, gate + 1):
-                x_wait(int(c > gate), k - 1, 1, peer).wait_recv()
+                    x_wait(0, 0, H - 1, 0, 0, gate + 1).wait_send()
+
+                x_wait(1, 0, H - 1, 0, gate + 1, NX).wait_send()
+            if k > 0 and c == 0:
+                x_wait(0, k - 1, 1, peer, 0, gate + 1).wait_recv()
+            if k > 0 and c > gate:
+                x_wait(c - gate, k - 1, 1, peer, c, c + 1).wait_recv()
             piece = jnp.concatenate(
                 [xbuf[peer, u].astype(F32) for u in range(xat[c], xat[c + 1])], axis=1
             )
@@ -398,7 +400,7 @@
     D = dl * H
     cols = w_tracks.shape[2]
     kvl = w_key.shape[1] + w_value.shape[1]
-    NC, NX = len(GROUPS), 3
+    NC, NX = len(GROUPS), 4 if dl >= 4 * 128 else 3
     vm = pl.BlockSpec(memory_space=pltpu.VMEM)
     hbm = pl.BlockSpec(memory_space=pl.ANY)
     dma = pltpu.SemaphoreType.DMA

time: 26.3 us -> 26.3 us (level)
  no operation moved by 1% of the time
where the time goes in v6:
time: 26.3 us; the launch traced here: 26.1 us
  Pallas kernels  25.4 us (97%)
  local copies, waits for them, and re-layouts  0.75 us (3%)
    pallas_call x1, Pallas kernels, body(): pl.pallas_call(functools.partial(kernel, H, N, NC, NX), out_shape=pltpu.V...  25.4 us
    unnamed x1, local copies, waits for them, and re-layouts  0.75 us

profile of v6, /device:TPU:0, one launch (start us, length us, event | category | flops | bytes accessed | tf_op | source)
XLA Modules:
  0.0 26.1 jit_solution(12857426448700730219)
XLA Ops:
  0.0 25.4 %shard_map.100 = f32[128,768]{1,0:T(8,128)S(1)} custom-call(s32[128,128]{1,0:T(8,128)} %bitcast.8, bf16[512,768]{1,0:T(8,128)(2,1)} %et_hbm.1, f32[12,128]{1,0:T(8,128)} %bitcast.9, bf16[1536,512]{1,0:T(8,128)(2,1)} %wq_hbm.1, bf16[64,1536]{1,0:T(8,128)(2,1)} %bitcast.7, bf16[96,1536]{1,0:T(8,128)(2,1)} %bitcast.6, bf16[768,1536]{1,0:T(8,128)(2,1)} %wo_hbm.1, ...), custom_call_target="tpu_custom_call" | custom-call | tf_op jit(solution)/shard_map/pallas_call | solution.py:408
  25.4 0.7 %copy.12 = f32[128,768]{1,0:T(8,128)} copy(f32[128,768]{1,0:T(8,128)S(1)} %shard_map.100) | data formatting | bytes 786432

commit v7 on v5

--- a/solution.py
+++ b/solution.py
@@ -16,7 +16,7 @@
 MESH = pl.DeviceIdType.MESH
 NT = (((1,), (1,)), ((), ()))
 FIRST = 1
-GROUPS = (2, 3, 3, 2, 2)
+GROUPS = (1, 3, 4, 3, 1)
 
 
 def spread(table, first, count):

time: 26.3 us -> 26.3 us (level)
  no operation moved by 1% of the time
where the time goes in v7:
time: 26.3 us; the launch traced here: 26.1 us
  Pallas kernels  25.4 us (97%)
  local copies, waits for them, and re-layouts  0.75 us (3%)
    pallas_call x1, Pallas kernels, body(): pl.pallas_call(functools.partial(kernel, H, N, NC, NX), out_shape=pltpu.V...  25.4 us
    unnamed x1, local copies, waits for them, and re-layouts  0.75 us

profile of v7, /device:TPU:0, one launch (start us, length us, event | category | flops | bytes accessed | tf_op | source)
XLA Modules:
  0.0 26.1 jit_solution(16447206895335519340)
XLA Ops:
  0.0 25.4 %shard_map.100 = f32[128,768]{1,0:T(8,128)S(1)} custom-call(s32[128,128]{1,0:T(8,128)} %bitcast.8, bf16[512,768]{1,0:T(8,128)(2,1)} %et_hbm.1, f32[12,128]{1,0:T(8,128)} %bitcast.9, bf16[1536,512]{1,0:T(8,128)(2,1)} %wq_hbm.1, bf16[64,1536]{1,0:T(8,128)(2,1)} %bitcast.7, bf16[96,1536]{1,0:T(8,128)(2,1)} %bitcast.6, bf16[768,1536]{1,0:T(8,128)(2,1)} %wo_hbm.1, ...), custom_call_target="tpu_custom_call" | custom-call | tf_op jit(solution)/shard_map/pallas_call | solution.py:406
  25.4 0.7 %copy.12 = f32[128,768]{1,0:T(8,128)} copy(f32[128,768]{1,0:T(8,128)S(1)} %shard_map.100) | data formatting | bytes 786432
